TPU v7x, 256 devices: a whole 4x4x8 slice. The times are simulated.
256 devices in a mesh: gx: 4 (over x), gy: 2 (over y_lo), ga: 32 (over y_hi, z, core).
Axes of the slice: x: 4, y: 4 (y_hi: 2, y_lo: 2; y = y_hi * 2 + y_lo), z: 8, core: 2. Of those that a mesh axis runs over, the one named last changes fastest.
Arguments:
- noise: float32 [128, 16, 256, 256], P('ga', None, 'gx', 'gy'), may hold values from 0 to 0.15
- labels: int32 [16, 256, 256], P(None, 'gx', 'gy'), may hold values from 0 to 127
- pair_class: int32 [128, 128], replicated, may hold values from 0 to 3
- class_gain: float32 [4], replicated, may hold values from 0.5 to 2
- stiffness: float32 [3, 128], P(None, 'ga'), may hold values from 0.5 to 1
- cross: float32 [128], P('ga'), may hold values from -0.4 to 0.4
- current: float32 [3, 16, 256, 256], P(None, None, 'gx', 'gy'), may hold values from -3 to 3
Outputs:
- order_out: float32 [128, 16, 256, 256], P('ga', None, 'gx', 'gy')
All inputs are finite; a program needn't handle non-finite values.
Results may differ from a plain program's by a relative error of at most 0.0011.
Values may be sent and summed in bfloat16 or wider, within the bound.
A program may use at most 128 MiB of HBM per device.

v0:
```python
import functools

import jax
import jax.numpy as jnp
from jax import lax
from jax.experimental import pallas as pl
from jax.experimental.pallas import tpu as pltpu
from jax.sharding import PartitionSpec as P

MESH = pl.DeviceIdType.MESH
seed_level = 0.7

PEERS, LAYERS, CHUNKS, DEPTH = 32, 16, 4, 4
ROWS, COLS = 32, 8
NOISE_TOP = 0.15
IN_SCALE = 32767.0 / NOISE_TOP
CODE_S = 2.0**-10
CODE_K = 32767.0 / 23.0
DIRS = ((0, -1), (0, 1), (-1, 0), (1, 0), (-1, -1), (-1, 1), (1, -1), (1, 1))
RIM_ROWS = (128, 128, 32, 32, 16, 16, 16, 16)
RIM_AT = (0, 128, 256, 288, 320, 336, 352, 368)
RIM_TOTAL = 384
RIM_BASE = (0, 4, 9)
RIM_SLOTS = 14


def exchange_kernel(
    n_gx,
    n_gy,
    noise_hbm,
    labels_hbm,
    class_ref,
    gain_ref,
    stiff_ref,
    cross_ref,
    current_hbm,
    out_hbm,
    noise,
    labels,
    current,
    outv,
    send_in,
    recv_in,
    send_out,
    recv_out,
    plane,
    field,
    drift,
    rim_send,
    rim_recv,
    coef_recv,
    coef_send,
    coef,
    pair_ref,
    load_sem,
    store_sem,
    in_send_sem,
    in_recv_sem,
    out_send_sem,
    out_recv_sem,
    rim_send_sem,
    rim_recv_sem,
    coef_send_sem,
    coef_recv_sem,
):
    gx, gy, ga = lax.axis_index("gx"), lax.axis_index("gy"), lax.axis_index("ga")
    sx, sy = ga // 16, ga % 16

    def neighbour(dx, dy):
        to_gx, to_gy, to_sx, to_sy = gx, gy, sx, sy
        if dx:
            to_sx = 1 - sx
            to_gx = (gx + sx) % n_gx if dx > 0 else (gx + n_gx - 1 + sx) % n_gx
        if dy > 0:
            to_sy = (sy + 1) % 16
            to_gy = (gy + (sy + 1) // 16) % n_gy
        if dy < 0:
            to_sy = (sy + 15) % 16
            to_gy = (gy + n_gy - 1 + (sy + 15) // 16) % n_gy
        return to_gx, to_gy, to_sx * 16 + to_sy

    def peer(k):
        return (gx, gy, (ga + k) % PEERS)

    def noise_load(c):
        at = pl.ds(c * DEPTH, DEPTH)
        return pltpu.make_async_copy(noise_hbm.at[:, at], noise.at[:, at], load_sem.at[c])

    half = pl.ds(pl.multiple_of(sx * ROWS, ROWS), ROWS)
    labels_load = pltpu.make_async_copy(labels_hbm.at[:, half], labels, load_sem.at[4])
    current_load = pltpu.make_async_copy(current_hbm.at[:, :, half], current, load_sem.at[5])
    for c in range(CHUNKS):
        noise_load(c).start()
    labels_load.start()
    current_load.start()

    barrier = pltpu.get_barrier_semaphore()

    def greet(k, _):
        pl.semaphore_signal(barrier, inc=1, device_id=peer(k), device_id_type=MESH)
        return 0

    lax.fori_loop(1, PEERS, greet, 0)
    for dx, dy in DIRS:
        pl.semaphore_signal(barrier, inc=1, device_id=neighbour(dx, dy), device_id_type=MESH)

    lane = lax.broadcasted_iota(jnp.int32, (1, 128), 1)
    rows = []
    for r in range(4):
        row = jnp.zeros((1, 128), jnp.float32)
        for k in range(4):
            value = stiff_ref[r, k] if r < 3 else cross_ref[k]
            row = jnp.where(lane == ga * 4 + k, value, row)
        rows.append(row)
    coef_send[...] = jnp.concatenate(rows + [jnp.zeros((4, 128), jnp.float32)], axis=0)

    def encode_in(c):
        for side in range(2):
            for gp in range(2):
                parts = []
                for g in (2 * gp, 2 * gp + 1):
                    block = noise[g, pl.ds(c * DEPTH, DEPTH), side * ROWS : (side + 1) * ROWS, :]
                    code = jnp.round(block.reshape(128, 128).T * IN_SCALE)
                    parts.append(code.reshape(16, 8, 128))
                both = jnp.concatenate(parts, axis=1).astype(jnp.int32).astype(jnp.int16)
                send_in[c, side * 16 : side * 16 + 16, gp * 16 : gp * 16 + 16, :] = both

    noise_load(0).wait()
    encode_in(0)
    pl.semaphore_wait(barrier, PEERS - 1 + len(DIRS))

    def start_coef(k, _):
        pltpu.make_async_remote_copy(
            coef_send, coef_recv.at[ga], coef_send_sem, coef_recv_sem, device_id=peer(k), device_id_type=MESH
        ).start()
        return 0

    lax.fori_loop(1, PEERS, start_coef, 0)
    pltpu.make_async_copy(coef_send, coef_recv.at[ga], coef_recv_sem).start()

    def start_in(c):
        def one(k, _):
            to = (ga + k) % PEERS
            pltpu.make_async_remote_copy(
                send_in.at[c, to], recv_in.at[c, ga], in_send_sem, in_recv_sem.at[c],
                device_id=(gx, gy, to), device_id_type=MESH,
            ).start()
            return 0

        lax.fori_loop(1, PEERS, one, 0)
        pltpu.make_async_copy(send_in.at[c, ga], recv_in.at[c, ga], in_recv_sem.at[c]).start()

    start_in(0)
    for c in range(1, CHUNKS):
        noise_load(c).wait()
        encode_in(c)
        start_in(c)

    picked = jnp.zeros((128, 128), jnp.float32)
    for k in range(4):
        picked = jnp.where(class_ref[...] == k, gain_ref[k], picked)
    row_id = lax.broadcasted_iota(jnp.int32, (128, 128), 0)
    col_id = lax.broadcasted_iota(jnp.int32, (128, 128), 1)
    symmetric = jnp.where(row_id == col_id, 0.0, 0.5 * (picked + picked.T))
    pair_ref[...] = (symmetric.astype(jnp.bfloat16).astype(jnp.float32) * 2.0).astype(jnp.bfloat16)

    labels_load.wait()
    current_load.wait()
    shift = (128 - sy * COLS) % 128
    grain = lax.broadcasted_iota(jnp.int32, (ROWS, 128), 1)

    def spread(z, _):
        own = pltpu.roll(labels[z], shift, 1)
        for y in range(COLS):
            column = jnp.broadcast_to(own[:, y : y + 1], (ROWS, 128))
            field[0, z * 10 + y + 1, 8:40, :] = jnp.where(column == grain, seed_level, 0.0)
        for k in range(3):
            flow = pltpu.roll(current[k, z] * 0.05, shift, 1)
            for y in range(COLS):
                drift[k, z * COLS + y] = jnp.broadcast_to(flow[:, y : y + 1], (ROWS, 128))
        return 0

    lax.fori_loop(0, LAYERS, spread, 0)

    pltpu.make_async_copy(coef_recv, coef_recv, coef_recv_sem).wait()
    total = jnp.sum(coef_recv[...], axis=0)
    k_x, k_y, k_z, k_xy = (jnp.broadcast_to(total[r : r + 1], (8, 128)) for r in range(4))
    coef[0] = 1.1 - 0.2 * (k_x + k_y + k_z)
    coef[1] = 0.1 * k_x
    coef[2] = 0.1 * k_y
    coef[3] = 0.1 * k_z
    coef[4] = 0.05 * k_xy

    def arrive(c):
        pltpu.make_async_copy(recv_in.at[c], recv_in.at[c], in_recv_sem.at[c]).wait()
        for p in range(0, PEERS, 4):
            block = recv_in[c, p : p + 4].astype(jnp.int32).astype(jnp.float32) * (1.0 / IN_SCALE)
            plane[p * 32 : (p + 4) * 32, :] = block.reshape(128, 128)
        for y in range(COLS):
            block = plane[pl.ds(y, 128, stride=8), :].T
            for d in range(DEPTH):
                at = (c * DEPTH + d) * 10 + y + 1
                field[0, at, 8:40, :] = field[0, at, 8:40, :] + block[d * ROWS : (d + 1) * ROWS]

    def layer_of(c, s, d):
        return jnp.clip(c * DEPTH - s + d, 0, LAYERS - 1)

    def rim_copies(s, c):
        slot = RIM_BASE[s] + c
        for n, (dx, dy) in enumerate(DIRS):
            m = DIRS.index((-dx, -dy))
            yield pltpu.make_async_remote_copy(
                rim_send.at[slot, pl.ds(RIM_AT[n], RIM_ROWS[n])], rim_recv.at[slot, pl.ds(RIM_AT[m], RIM_ROWS[m])],
                rim_send_sem, rim_recv_sem.at[slot], device_id=neighbour(dx, dy), device_id_type=MESH,
            )

    flat = field.reshape(4, LAYERS * 10 * 48, 128)

    def send_rims(s, c):
        slot = RIM_BASE[s] + c
        layers = [layer_of(c, s, d) for d in range(DEPTH)]
        for d, z in enumerate(layers):
            rim_send[slot, d * ROWS : (d + 1) * ROWS, :] = field[s, z * 10 + 1, 8:40, :].astype(jnp.bfloat16)
            rim_send[slot, 128 + d * ROWS : 128 + (d + 1) * ROWS, :] = field[s, z * 10 + 8, 8:40, :].astype(jnp.bfloat16)
        for n, x in ((2, 8), (3, 39)):
            for d in range(0, DEPTH, 2):
                pieces = [flat[s, pl.ds((layers[e] * 10 + 1) * 48 + x, COLS, stride=48), :] for e in (d, d + 1)]
                at = RIM_AT[n] + d * COLS
                rim_send[slot, at : at + 16, :] = jnp.concatenate(pieces, axis=0).astype(jnp.bfloat16)
        for n, (y, x) in ((4, (1, 8)), (5, (8, 8)), (6, (1, 39)), (7, (8, 39))):
            pieces = [field[s, z * 10 + y, x : x + 1, :] for z in layers] + [jnp.zeros((12, 128), jnp.float32)]
            rim_send[slot, RIM_AT[n] : RIM_AT[n] + 16, :] = jnp.concatenate(pieces, axis=0).astype(jnp.bfloat16)
        for copy in rim_copies(s, c):
            copy.start()

    def take_rims(s, c):
        slot = RIM_BASE[s] + c
        pltpu.make_async_copy(rim_recv.at[slot], rim_recv.at[slot], rim_recv_sem.at[slot]).wait()
        layers = [layer_of(c, s, d) for d in range(DEPTH)]
        for d, z in enumerate(layers):
            field[s, z * 10, 8:40, :] = rim_recv[slot, d * ROWS : (d + 1) * ROWS, :].astype(jnp.float32)
            field[s, z * 10 + 9, 8:40, :] = rim_recv[slot, 128 + d * ROWS : 128 + (d + 1) * ROWS, :].astype(jnp.float32)
        for n, x in ((2, 7), (3, 40)):
            for d in range(0, DEPTH, 2):
                at = RIM_AT[n] + d * COLS
                pieces = rim_recv[slot, at : at + 16, :].astype(jnp.float32)
                for e in (0, 1):
                    flat[s, pl.ds((layers[d + e] * 10 + 1) * 48 + x, COLS, stride=48), :] = pieces[e * 8 : e * 8 + 8]
        for n, (y, x) in ((4, (0, 7)), (5, (9, 7)), (6, (0, 40)), (7, (9, 40))):
            pieces = rim_recv[slot, RIM_AT[n] : RIM_AT[n] + 16, :].astype(jnp.float32)
            for d, z in enumerate(layers):
                field[s, z * 10 + y, x : x + 1, :] = pieces[d : d + 1]

    def step(s, c):
        def one(z, _):
            here = z * 10
            above = jnp.minimum(z + 1, LAYERS - 1) * 10
            below = jnp.maximum(z - 1, 0) * 10
            squares = [jnp.square(field[s - 1, here + y + 1, 8:40, :]).astype(jnp.bfloat16) for y in range(COLS)]
            twice = jnp.dot(jnp.concatenate(squares, axis=0), pair_ref[...], preferred_element_type=jnp.float32)

            def wide(n):
                return jnp.concatenate([coef[n]] * 4, axis=0)

            a_0, a_x, a_y, a_z, a_xy = (wide(n) for n in range(5))

            def slope(y):
                return field[s - 1, here + y + 1, 9:41, :] - field[s - 1, here + y + 1, 7:39, :]

            slopes = [slope(-1), slope(0)]
            for y in range(COLS):
                slopes.append(slope(y + 1))
                v = field[s - 1, here + y + 1, 8:40, :]
                x_p, x_m = field[s - 1, here + y + 1, 9:41, :], field[s - 1, here + y + 1, 7:39, :]
                y_p, y_m = field[s - 1, here + y + 2, 8:40, :], field[s - 1, here + y, 8:40, :]
                z_p, z_m = field[s - 1, above + y + 1, 8:40, :], field[s - 1, below + y + 1, 8:40, :]
                new = v * (a_0 - 0.1 * (v * v + twice[y * ROWS : (y + 1) * ROWS]))
                new = new + a_x * (x_p + x_m) + a_y * (y_p + y_m) + a_z * (z_p + z_m)
                new = new + a_xy * (slopes[y + 2] - slopes[y])
                at = z * COLS + y
                new = new - (drift[0, at] * slopes[y + 1] + drift[1, at] * (y_p - y_m) + drift[2, at] * (z_p - z_m))
                field[s, here + y + 1, 8:40, :] = new
            return 0

        first = jnp.maximum(c * DEPTH - s, 0)
        last = jnp.minimum(c * DEPTH - s + DEPTH, LAYERS)
        lax.fori_loop(first, last, one, 0)

    def leave(c):
        for y in range(COLS):
            parts = [field[3, (c * DEPTH + d) * 10 + y + 1, 8:40, :] for d in range(DEPTH)]
            plane[pl.ds(y, 128, stride=8), :] = jnp.concatenate(parts, axis=0).T
        for p in range(0, PEERS, 4):
            block = plane[p * 32 : (p + 4) * 32, :].reshape(4, 32, 128)
            level = jnp.minimum(jnp.round(CODE_K * jnp.log2(1.0 + jnp.abs(block) * (1.0 / CODE_S))), 32767.0)
            code = jnp.where(block < 0.0, -level, level)
            send_out[c, p : p + 4] = code.astype(jnp.int32).astype(jnp.int16)

        def one(k, _):
            to = (ga + k) % PEERS
            pltpu.make_async_remote_copy(
                send_out.at[c, to], recv_out.at[c, ga], out_send_sem, out_recv_sem.at[c],
                device_id=(gx, gy, to), device_id_type=MESH,
            ).start()
            return 0

        lax.fori_loop(1, PEERS, one, 0)
        pltpu.make_async_copy(send_out.at[c, ga], recv_out.at[c, ga], out_recv_sem.at[c]).start()

    def turn(i, _):
        @pl.when(i < CHUNKS)
        def _():
            arrive(i)
            send_rims(0, i)

        @pl.when(i >= 1)
        def _():
            take_rims(1, i - 1)
            step(2, i - 1)
            send_rims(2, i - 1)

        @pl.when(i < CHUNKS)
        def _():
            take_rims(0, i)

        @pl.when(i <= CHUNKS)
        def _():
            step(1, i)
            send_rims(1, i)

        @pl.when(i >= 1)
        def _():
            take_rims(2, i - 1)
            step(3, i - 1)

        @pl.when(i >= 2)
        def _():
            leave(i - 2)

        return 0

    lax.fori_loop(0, CHUNKS + 2, turn, 0)

    def store(c):
        at = pl.ds(c * DEPTH, DEPTH)
        return pltpu.make_async_copy(outv.at[:, at], out_hbm.at[:, at], store_sem.at[c])

    def finish(c, _):
        pltpu.make_async_copy(recv_out.at[c], recv_out.at[c], out_recv_sem.at[c]).wait()
        for side in range(2):
            for gp in range(2):
                code = recv_out[c, side * 16 : side * 16 + 16, gp * 16 : gp * 16 + 16, :]
                level = code.astype(jnp.int32).astype(jnp.float32) * (1.0 / CODE_K)
                size = jnp.exp2(jnp.abs(level)) * CODE_S - CODE_S
                value = jnp.where(level < 0.0, -size, size)
                for e in range(2):
                    block = value[:, e * 8 : e * 8 + 8, :].reshape(128, 128).T
                    outv[2 * gp + e, pl.ds(c * DEPTH, DEPTH), side * ROWS : (side + 1) * ROWS, :] = block.reshape(
                        DEPTH, ROWS, 128
                    )
        store(c).start()
        return 0

    lax.fori_loop(0, CHUNKS, finish, 0)
    for c in range(CHUNKS):
        store(c).wait()
    most = pl.ds(0, PEERS - 1)
    pltpu.make_async_copy(send_in.at[:, most], send_in.at[:, most], in_send_sem).wait()
    pltpu.make_async_copy(send_out.at[:, most], send_out.at[:, most], out_send_sem).wait()
    pltpu.make_async_copy(rim_send, rim_send, rim_send_sem).wait()
    pltpu.make_async_copy(coef_recv.at[most], coef_recv.at[most], coef_send_sem).wait()


def per_device(n_gx, n_gy, noise, labels, pair_class, class_gain, stiffness, cross, current):
    hbm = pl.BlockSpec(memory_space=pl.ANY)
    vmem = pl.BlockSpec(memory_space=pltpu.VMEM)
    smem = pl.BlockSpec(memory_space=pltpu.SMEM)
    dma = pltpu.SemaphoreType.DMA
    f32, bf16, i16 = jnp.float32, jnp.bfloat16, jnp.int16
    return pl.pallas_call(
        functools.partial(exchange_kernel, n_gx, n_gy),
        out_shape=jax.ShapeDtypeStruct(noise.shape, f32),
        in_specs=[hbm, hbm, vmem, smem, smem, smem, hbm],
        out_specs=hbm,
        scratch_shapes=[
            pltpu.VMEM((4, LAYERS, 64, 128), f32),
            pltpu.VMEM((LAYERS, ROWS, 128), jnp.int32),
            pltpu.VMEM((3, LAYERS, ROWS, 128), f32),
            pltpu.VMEM((4, LAYERS, 64, 128), f32),
            pltpu.VMEM((CHUNKS, PEERS, 32, 128), i16),
            pltpu.VMEM((CHUNKS, PEERS, 32, 128), i16),
            pltpu.VMEM((CHUNKS, PEERS, 32, 128), i16),
            pltpu.VMEM((CHUNKS, PEERS, 32, 128), i16),
            pltpu.VMEM((PEERS * 32, 128), f32),
            pltpu.VMEM((4, LAYERS * 10, 48, 128), f32),
            pltpu.VMEM((3, LAYERS * COLS, ROWS, 128), f32),
            pltpu.VMEM((RIM_SLOTS, RIM_TOTAL, 128), bf16),
            pltpu.VMEM((RIM_SLOTS, RIM_TOTAL, 128), bf16),
            pltpu.VMEM((PEERS, 8, 128), f32),
            pltpu.VMEM((8, 128), f32),
            pltpu.VMEM((5, 8, 128), f32),
            pltpu.VMEM((128, 128), bf16),
            dma((6,)),
            dma((CHUNKS,)),
            dma,
            dma((CHUNKS,)),
            dma,
            dma((CHUNKS,)),
            dma,
            dma((RIM_SLOTS,)),
            dma,
            dma,
        ],
        compiler_params=pltpu.CompilerParams(
            collective_id=0, has_side_effects=True, vmem_limit_bytes=60 * 1024 * 1024
        ),
        name="phase_steps",
    )(noise, labels, pair_class, class_gain, stiffness, cross, current)


def solution(mesh):
    placed = (
        P("ga", None, "gx", "gy"),
        P(None, "gx", "gy"),
        P(),
        P(),
        P(None, "ga"),
        P("ga"),
        P(None, None, "gx", "gy"),
    )
    return jax.shard_map(
        functools.partial(per_device, mesh.shape["gx"], mesh.shape["gy"]),
        mesh=mesh,
        in_specs=placed,
        out_specs=P("ga", None, "gx", "gy"),
        check_vma=False,
    )
```

profile of v0, /device:TPU:1, one launch (start us, length us, event | category | flops | bytes accessed | tf_op | source)
XLA Modules:
  0.0 111.6 jit_solution(4508188231430494275)
XLA Ops:
  0.0 108.4 %phase_steps.1 = f32[4,16,64,128]{3,2,1,0:T(8,128)} custom-call(f32[4,16,64,128]{3,2,1,0:T(8,128)} %noise_hbm.1, s32[16,64,128]{2,1,0:T(8,128)} %labels_hbm.1, s32[128,128]{1,0:T(8,128)} %class_ref.1, f32[4]{0:T(128)} %gain_ref.1, f32[3,4]{1,0:T(4,128)} %stiff_ref.1, f32[4]{0:T(128)} %cross_ref.1, f32[3,16,64,128]{3,2,1,0:T(8,128)} %current_hbm.1), custom_call_target="tpu_custom_call" | custom-call | tf_op jit(solution)/shard_map/phase_steps/pallas_call | solution.py:380
  108.4 3.2 %copy.9 = f32[4,16,64,128]{3,2,1,0:T(8,128)} copy(f32[4,16,64,128]{3,2,1,0:T(8,128)} %phase_steps.1) | data formatting | bytes 4194304
where the time goes:
time: 112 us
  Pallas kernels  108 us (96%)
  local copies, waits for them, and re-layouts  3.16 us (3%)
    pallas_call x1, Pallas kernels, per_device(): pl.pallas_call(functools.partial(exchange_kernel, n_gx, n_gy), out_shape=...  108 us
    unnamed x1, local copies, waits for them, and re-layouts  3.16 us

commit v1 on v0

--- a/solution.py
+++ b/solution.py
@@ -112,7 +112,7 @@
             value = stiff_ref[r, k] if r < 3 else cross_ref[k]
             row = jnp.where(lane == ga * 4 + k, value, row)
         rows.append(row)
-    coef_send[...] = jnp.concatenate(rows + [jnp.zeros((4, 128), jnp.float32)], axis=0)
+    coef_send[0] = jnp.concatenate(rows + [jnp.zeros((4, 128), jnp.float32)], axis=0)
 
     def encode_in(c):
         for side in range(2):
@@ -129,32 +129,45 @@
     encode_in(0)
     pl.semaphore_wait(barrier, PEERS - 1 + len(DIRS))
 
-    def start_coef(k, _):
-        pltpu.make_async_remote_copy(
-            coef_send, coef_recv.at[ga], coef_send_sem, coef_recv_sem, device_id=peer(k), device_id_type=MESH
-        ).start()
-        return 0
-
-    lax.fori_loop(1, PEERS, start_coef, 0)
-    pltpu.make_async_copy(coef_send, coef_recv.at[ga], coef_recv_sem).start()
-
-    def start_in(c):
+    chip = sy // 2
+
+    def coef_first(k):
+        to = sx * 16 + ((chip + k) % 8) * 2 + sy % 2
+        return pltpu.make_async_remote_copy(
+            coef_send.at[0], coef_recv.at[0, chip], coef_send_sem.at[0], coef_recv_sem.at[0],
+            device_id=(gx, gy, to), device_id_type=MESH,
+        )
+
+    group = sx * 2 + sy % 2
+
+    def coef_second(k):
+        to = (group + k) % 4
+        return pltpu.make_async_remote_copy(
+            coef_send.at[1], coef_recv.at[1, group], coef_send_sem.at[1], coef_recv_sem.at[1],
+            device_id=(gx, gy, (to // 2) * 16 + chip * 2 + to % 2), device_id_type=MESH,
+        )
+
+    for k in range(1, 8):
+        coef_first(k).start()
+    pltpu.make_async_copy(coef_send.at[0], coef_recv.at[0, chip], coef_recv_sem.at[0]).start()
+
+    def swap(send, recv, send_sem, recv_sem, c):
         def one(k, _):
             to = (ga + k) % PEERS
             pltpu.make_async_remote_copy(
-                send_in.at[c, to], recv_in.at[c, ga], in_send_sem, in_recv_sem.at[c],
+                send.at[c, to], recv.at[c, ga], send_sem, recv_sem.at[c],
                 device_id=(gx, gy, to), device_id_type=MESH,
             ).start()
             return 0
 
         lax.fori_loop(1, PEERS, one, 0)
-        pltpu.make_async_copy(send_in.at[c, ga], recv_in.at[c, ga], in_recv_sem.at[c]).start()
-
-    start_in(0)
+        pltpu.make_async_copy(send.at[c, ga], recv.at[c, ga], recv_sem.at[c]).start()
+
+    swap(send_in, recv_in, in_send_sem, in_recv_sem, 0)
     for c in range(1, CHUNKS):
         noise_load(c).wait()
         encode_in(c)
-        start_in(c)
+        swap(send_in, recv_in, in_send_sem, in_recv_sem, c)
 
     picked = jnp.zeros((128, 128), jnp.float32)
     for k in range(4):
@@ -180,10 +193,17 @@
                 drift[k, z * COLS + y] = jnp.broadcast_to(flow[:, y : y + 1], (ROWS, 128))
         return 0
 
+    pltpu.make_async_copy(coef_recv.at[0], coef_recv.at[0], coef_recv_sem.at[0]).wait()
+    coef_send[1] = jnp.sum(coef_recv[0], axis=0)
+    for k in range(1, 4):
+        coef_second(k).start()
+    pltpu.make_async_copy(coef_send.at[1], coef_recv.at[1, group], coef_recv_sem.at[1]).start()
+
     lax.fori_loop(0, LAYERS, spread, 0)
 
-    pltpu.make_async_copy(coef_recv, coef_recv, coef_recv_sem).wait()
-    total = jnp.sum(coef_recv[...], axis=0)
+    quarter = coef_recv.at[1, pl.ds(0, 4)]
+    pltpu.make_async_copy(quarter, quarter, coef_recv_sem.at[1]).wait()
+    total = jnp.sum(coef_recv[1, 0:4], axis=0)
     k_x, k_y, k_z, k_xy = (jnp.broadcast_to(total[r : r + 1], (8, 128)) for r in range(4))
     coef[0] = 1.1 - 0.2 * (k_x + k_y + k_z)
     coef[1] = 0.1 * k_x
@@ -296,50 +316,41 @@
             code = jnp.where(block < 0.0, -level, level)
             send_out[c, p : p + 4] = code.astype(jnp.int32).astype(jnp.int16)
 
-        def one(k, _):
-            to = (ga + k) % PEERS
-            pltpu.make_async_remote_copy(
-                send_out.at[c, to], recv_out.at[c, ga], out_send_sem, out_recv_sem.at[c],
-                device_id=(gx, gy, to), device_id_type=MESH,
-            ).start()
-            return 0
-
-        lax.fori_loop(1, PEERS, one, 0)
-        pltpu.make_async_copy(send_out.at[c, ga], recv_out.at[c, ga], out_recv_sem.at[c]).start()
-
-    def turn(i, _):
-        @pl.when(i < CHUNKS)
+    def start(c, _):
+        arrive(c)
+        send_rims(0, c)
+        return 0
+
+    lax.fori_loop(0, CHUNKS, start, 0)
+
+    def first(c, _):
+        @pl.when(c < CHUNKS)
         def _():
-            arrive(i)
-            send_rims(0, i)
-
-        @pl.when(i >= 1)
+            take_rims(0, c)
+
+        step(1, c)
+        send_rims(1, c)
+        return 0
+
+    def second(c, _):
+        take_rims(1, c)
+        step(2, c)
+        send_rims(2, c)
+        return 0
+
+    def third(c, _):
+        take_rims(2, c)
+        step(3, c)
+
+        @pl.when(c >= 1)
         def _():
-            take_rims(1, i - 1)
-            step(2, i - 1)
-            send_rims(2, i - 1)
-
-        @pl.when(i < CHUNKS)
-        def _():
-            take_rims(0, i)
-
-        @pl.when(i <= CHUNKS)
-        def _():
-            step(1, i)
-            send_rims(1, i)
-
-        @pl.when(i >= 1)
-        def _():
-            take_rims(2, i - 1)
-            step(3, i - 1)
-
-        @pl.when(i >= 2)
-        def _():
-            leave(i - 2)
-
-        return 0
-
-    lax.fori_loop(0, CHUNKS + 2, turn, 0)
+            leave(c - 1)
+            swap(send_out, recv_out, out_send_sem, out_recv_sem, c - 1)
+
+        return 0
+
+    for phase in (first, second, third):
+        lax.fori_loop(0, CHUNKS + 1, phase, 0)
 
     def store(c):
         at = pl.ds(c * DEPTH, DEPTH)
@@ -350,11 +361,9 @@
         for side in range(2):
             for gp in range(2):
                 code = recv_out[c, side * 16 : side * 16 + 16, gp * 16 : gp * 16 + 16, :]
-                level = code.astype(jnp.int32).astype(jnp.float32) * (1.0 / CODE_K)
-                size = jnp.exp2(jnp.abs(level)) * CODE_S - CODE_S
-                value = jnp.where(level < 0.0, -size, size)
+                level = code.astype(jnp.int32).astype(jnp.float32)
                 for e in range(2):
-                    block = value[:, e * 8 : e * 8 + 8, :].reshape(128, 128).T
+                    block = level[:, e * 8 : e * 8 + 8, :].reshape(128, 128).T.astype(jnp.int32).astype(jnp.int16)
                     outv[2 * gp + e, pl.ds(c * DEPTH, DEPTH), side * ROWS : (side + 1) * ROWS, :] = block.reshape(
                         DEPTH, ROWS, 128
                     )
@@ -368,7 +377,9 @@
     pltpu.make_async_copy(send_in.at[:, most], send_in.at[:, most], in_send_sem).wait()
     pltpu.make_async_copy(send_out.at[:, most], send_out.at[:, most], out_send_sem).wait()
     pltpu.make_async_copy(rim_send, rim_send, rim_send_sem).wait()
-    pltpu.make_async_copy(coef_recv.at[most], coef_recv.at[most], coef_send_sem).wait()
+    for n, count in ((0, 7), (1, 3)):
+        sent = coef_recv.at[0, pl.ds(0, count)]
+        pltpu.make_async_copy(sent, sent, coef_send_sem.at[n]).wait()
 
 
 def per_device(n_gx, n_gy, noise, labels, pair_class, class_gain, stiffness, cross, current):
@@ -377,16 +388,16 @@
     smem = pl.BlockSpec(memory_space=pltpu.SMEM)
     dma = pltpu.SemaphoreType.DMA
     f32, bf16, i16 = jnp.float32, jnp.bfloat16, jnp.int16
-    return pl.pallas_call(
+    code = pl.pallas_call(
         functools.partial(exchange_kernel, n_gx, n_gy),
-        out_shape=jax.ShapeDtypeStruct(noise.shape, f32),
+        out_shape=jax.ShapeDtypeStruct(noise.shape, i16),
         in_specs=[hbm, hbm, vmem, smem, smem, smem, hbm],
         out_specs=hbm,
         scratch_shapes=[
             pltpu.VMEM((4, LAYERS, 64, 128), f32),
             pltpu.VMEM((LAYERS, ROWS, 128), jnp.int32),
             pltpu.VMEM((3, LAYERS, ROWS, 128), f32),
-            pltpu.VMEM((4, LAYERS, 64, 128), f32),
+            pltpu.VMEM((4, LAYERS, 64, 128), i16),
             pltpu.VMEM((CHUNKS, PEERS, 32, 128), i16),
             pltpu.VMEM((CHUNKS, PEERS, 32, 128), i16),
             pltpu.VMEM((CHUNKS, PEERS, 32, 128), i16),
@@ -396,8 +407,8 @@
             pltpu.VMEM((3, LAYERS * COLS, ROWS, 128), f32),
             pltpu.VMEM((RIM_SLOTS, RIM_TOTAL, 128), bf16),
             pltpu.VMEM((RIM_SLOTS, RIM_TOTAL, 128), bf16),
-            pltpu.VMEM((PEERS, 8, 128), f32),
-            pltpu.VMEM((8, 128), f32),
+            pltpu.VMEM((2, 8, 8, 128), f32),
+            pltpu.VMEM((2, 8, 128), f32),
             pltpu.VMEM((5, 8, 128), f32),
             pltpu.VMEM((128, 128), bf16),
             dma((6,)),
@@ -408,14 +419,17 @@
             dma((CHUNKS,)),
             dma,
             dma((RIM_SLOTS,)),
-            dma,
-            dma,
+            dma((2,)),
+            dma((2,)),
         ],
         compiler_params=pltpu.CompilerParams(
             collective_id=0, has_side_effects=True, vmem_limit_bytes=60 * 1024 * 1024
         ),
         name="phase_steps",
     )(noise, labels, pair_class, class_gain, stiffness, cross, current)
+    level = code.astype(f32) * (1.0 / CODE_K)
+    size = jnp.exp2(jnp.abs(level)) * CODE_S - CODE_S
+    return jnp.where(level < 0.0, -size, size)
 
 
 def solution(mesh):

time: 112 us -> 85 us (0.76)
  Pallas kernels: 108 us -> 81.3 us
  other arithmetic: 0 us -> 3.5 us
  local copies, waits for them, and re-layouts: 3.16 us -> 0 us
    pallas_call x1, Pallas kernels: 108 us -> 81.3 us  [per_device(): pl.pallas_call(functools.partial(exchange_kernel, n_gx, n_gy), out_shape=...]
    select_n x0 -> x1, other arithmetic: none -> 3.5 us  [per_device(): return jnp.where(level < 0.0, -size, size)]
    unnamed x1 -> x0, local copies, waits for them, and re-layouts: 3.16 us -> none
where the time goes in v1:
time: 85 us; the launch traced here: 84.8 us
  Pallas kernels  81.3 us (96%)
  other arithmetic  3.5 us (4%)
    pallas_call x1, Pallas kernels, per_device(): pl.pallas_call(functools.partial(exchange_kernel, n_gx, n_gy), out_shape=...  81.3 us
    select_n x1, other arithmetic, per_device(): return jnp.where(level < 0.0, -size, size)  3.5 us

profile of v1, /device:TPU:1, one launch (start us, length us, event | category | flops | bytes accessed | tf_op | source)
XLA Modules:
  0.0 84.8 jit_solution(9713383881493117387)
XLA Ops:
  0.0 81.3 %phase_steps.1 = s16[4,16,64,128]{3,2,1,0:T(8,128)(2,1)} custom-call(f32[4,16,64,128]{3,2,1,0:T(8,128)} %noise_hbm.1, s32[16,64,128]{2,1,0:T(8,128)} %labels_hbm.1, s32[128,128]{1,0:T(8,128)} %class_ref.1, f32[4]{0:T(128)} %gain_ref.1, f32[3,4]{1,0:T(4,128)} %stiff_ref.1, f32[4]{0:T(128)} %cross_ref.1, f32[3,16,64,128]{3,2,1,0:T(8,128)} %current_hbm.1), custom_call_target="tpu_custom_call" | custom-call | tf_op jit(solution)/shard_map/phase_steps/pallas_call | solution.py:391
  81.3 3.5 %negate_select_fusion = f32[4,16,64,128]{3,2,1,0:T(8,128)} fusion(s16[4,16,64,128]{3,2,1,0:T(8,128)(2,1)} %phase_steps.1), kind=kLoop, calls=%fused_computation | loop fusion | flops 4718592 | bytes 3145728 | tf_op jit(solution)/shard_map/jit(_where)/select_n | solution.py:432

commit v2 on v1

--- a/solution.py
+++ b/solution.py
@@ -29,15 +29,19 @@
     n_gy,
     noise_hbm,
     labels_hbm,
-    class_ref,
-    gain_ref,
-    stiff_ref,
-    cross_ref,
+    class_hbm,
+    gain_hbm,
+    stiff_hbm,
+    cross_hbm,
     current_hbm,
     out_hbm,
     noise,
     labels,
     current,
+    class_ref,
+    gain_ref,
+    stiff_ref,
+    cross_ref,
     outv,
     send_in,
     recv_in,
@@ -89,7 +93,12 @@
     half = pl.ds(pl.multiple_of(sx * ROWS, ROWS), ROWS)
     labels_load = pltpu.make_async_copy(labels_hbm.at[:, half], labels, load_sem.at[4])
     current_load = pltpu.make_async_copy(current_hbm.at[:, :, half], current, load_sem.at[5])
-    for c in range(CHUNKS):
+    small = ((stiff_hbm, stiff_ref), (cross_hbm, cross_ref), (gain_hbm, gain_ref), (class_hbm, class_ref))
+    small_loads = [pltpu.make_async_copy(a, b, load_sem.at[6 + n]) for n, (a, b) in enumerate(small)]
+    noise_load(0).start()
+    for load in small_loads:
+        load.start()
+    for c in range(1, CHUNKS):
         noise_load(c).start()
     labels_load.start()
     current_load.start()
@@ -104,6 +113,8 @@
     for dx, dy in DIRS:
         pl.semaphore_signal(barrier, inc=1, device_id=neighbour(dx, dy), device_id_type=MESH)
 
+    small_loads[0].wait()
+    small_loads[1].wait()
     lane = lax.broadcasted_iota(jnp.int32, (1, 128), 1)
     rows = []
     for r in range(4):
@@ -167,8 +178,11 @@
     for c in range(1, CHUNKS):
         noise_load(c).wait()
         encode_in(c)
-        swap(send_in, recv_in, in_send_sem, in_recv_sem, c)
-
+        if c < CHUNKS - 1:
+            swap(send_in, recv_in, in_send_sem, in_recv_sem, c)
+
+    small_loads[2].wait()
+    small_loads[3].wait()
     picked = jnp.zeros((128, 128), jnp.float32)
     for k in range(4):
         picked = jnp.where(class_ref[...] == k, gain_ref[k], picked)
@@ -316,13 +330,6 @@
             code = jnp.where(block < 0.0, -level, level)
             send_out[c, p : p + 4] = code.astype(jnp.int32).astype(jnp.int16)
 
-    def start(c, _):
-        arrive(c)
-        send_rims(0, c)
-        return 0
-
-    lax.fori_loop(0, CHUNKS, start, 0)
-
     def first(c, _):
         @pl.when(c < CHUNKS)
         def _():
@@ -345,12 +352,36 @@
         @pl.when(c >= 1)
         def _():
             leave(c - 1)
+
+        @pl.when(c >= 2)
+        def _():
             swap(send_out, recv_out, out_send_sem, out_recv_sem, c - 1)
 
         return 0
 
-    for phase in (first, second, third):
-        lax.fori_loop(0, CHUNKS + 1, phase, 0)
+    def start(c, _):
+        arrive(c)
+        send_rims(0, c)
+
+        @pl.when(c == 1)
+        def _():
+            swap(send_in, recv_in, in_send_sem, in_recv_sem, CHUNKS - 1)
+
+        @pl.when(c == 2)
+        def _():
+            lax.fori_loop(0, 2, first, 0)
+
+        return 0
+
+    lax.fori_loop(0, CHUNKS, start, 0)
+    lax.fori_loop(2, 3, first, 0)
+    lax.fori_loop(0, 2, second, 0)
+    lax.fori_loop(3, CHUNKS + 1, first, 0)
+    lax.fori_loop(2, 3, second, 0)
+    lax.fori_loop(0, 2, third, 0)
+    lax.fori_loop(3, CHUNKS + 1, second, 0)
+    swap(send_out, recv_out, out_send_sem, out_recv_sem, 0)
+    lax.fori_loop(2, CHUNKS + 1, third, 0)
 
     def store(c):
         at = pl.ds(c * DEPTH, DEPTH)
@@ -384,19 +415,21 @@
 
 def per_device(n_gx, n_gy, noise, labels, pair_class, class_gain, stiffness, cross, current):
     hbm = pl.BlockSpec(memory_space=pl.ANY)
-    vmem = pl.BlockSpec(memory_space=pltpu.VMEM)
-    smem = pl.BlockSpec(memory_space=pltpu.SMEM)
     dma = pltpu.SemaphoreType.DMA
     f32, bf16, i16 = jnp.float32, jnp.bfloat16, jnp.int16
     code = pl.pallas_call(
         functools.partial(exchange_kernel, n_gx, n_gy),
         out_shape=jax.ShapeDtypeStruct(noise.shape, i16),
-        in_specs=[hbm, hbm, vmem, smem, smem, smem, hbm],
+        in_specs=[hbm] * 7,
         out_specs=hbm,
         scratch_shapes=[
             pltpu.VMEM((4, LAYERS, 64, 128), f32),
             pltpu.VMEM((LAYERS, ROWS, 128), jnp.int32),
             pltpu.VMEM((3, LAYERS, ROWS, 128), f32),
+            pltpu.VMEM((128, 128), jnp.int32),
+            pltpu.SMEM((4,), f32),
+            pltpu.SMEM((3, 4), f32),
+            pltpu.SMEM((4,), f32),
             pltpu.VMEM((4, LAYERS, 64, 128), i16),
             pltpu.VMEM((CHUNKS, PEERS, 32, 128), i16),
             pltpu.VMEM((CHUNKS, PEERS, 32, 128), i16),
@@ -411,7 +444,7 @@
             pltpu.VMEM((2, 8, 128), f32),
             pltpu.VMEM((5, 8, 128), f32),
             pltpu.VMEM((128, 128), bf16),
-            dma((6,)),
+            dma((10,)),
             dma((CHUNKS,)),
             dma,
             dma((CHUNKS,)),

time: 85 us -> 82.4 us (0.969)
  Pallas kernels: 81.3 us -> 78.8 us
    pallas_call x1, Pallas kernels: 81.3 us -> 78.8 us  [per_device(): pl.pallas_call(functools.partial(exchange_kernel, n_gx, n_gy), out_shape=...]
where the time goes in v2:
time: 82.4 us; the launch traced here: 82.3 us
  Pallas kernels  78.8 us (96%)
  other arithmetic  3.5 us (4%)
    pallas_call x1, Pallas kernels, per_device(): pl.pallas_call(functools.partial(exchange_kernel, n_gx, n_gy), out_shape=...  78.8 us
    select_n x1, other arithmetic, per_device(): return jnp.where(level < 0.0, -size, size)  3.5 us

profile of v2, /device:TPU:1, one launch (start us, length us, event | category | flops | bytes accessed | tf_op | source)
XLA Modules:
  0.0 82.3 jit_solution(1961107300859976847)
XLA Ops:
  0.0 78.8 %phase_steps.1 = s16[4,16,64,128]{3,2,1,0:T(8,128)(2,1)} custom-call(f32[4,16,64,128]{3,2,1,0:T(8,128)} %noise_hbm.1, s32[16,64,128]{2,1,0:T(8,128)} %labels_hbm.1, s32[128,128]{1,0:T(8,128)} %class_hbm.1, f32[4]{0:T(128)} %gain_hbm.1, f32[3,4]{1,0:T(4,128)} %stiff_hbm.1, f32[4]{0:T(128)} %cross_hbm.1, f32[3,16,64,128]{3,2,1,0:T(8,128)} %current_hbm.1), custom_call_target="tpu_custom_call" | custom-call | tf_op jit(solution)/shard_map/phase_steps/pallas_call | solution.py:420
  78.8 3.5 %negate_select_fusion = f32[4,16,64,128]{3,2,1,0:T(8,128)} fusion(s16[4,16,64,128]{3,2,1,0:T(8,128)(2,1)} %phase_steps.1), kind=kLoop, calls=%fused_computation | loop fusion | flops 4718592 | bytes 3145728 | tf_op jit(solution)/shard_map/jit(_where)/select_n | solution.py:465

commit v3 on v2

--- a/solution.py
+++ b/solution.py
@@ -50,6 +50,7 @@
     plane,
     field,
     drift,
+    sums,
     rim_send,
     rim_recv,
     coef_recv,
@@ -241,7 +242,8 @@
 
     def rim_copies(s, c):
         slot = RIM_BASE[s] + c
-        for n, (dx, dy) in enumerate(DIRS):
+        for n in (4, 5, 6, 7, 2, 3, 0, 1):
+            dx, dy = DIRS[n]
             m = DIRS.index((-dx, -dy))
             yield pltpu.make_async_remote_copy(
                 rim_send.at[slot, pl.ds(RIM_AT[n], RIM_ROWS[n])], rim_recv.at[slot, pl.ds(RIM_AT[m], RIM_ROWS[m])],
@@ -285,13 +287,18 @@
             for d, z in enumerate(layers):
                 field[s, z * 10 + y, x : x + 1, :] = pieces[d : d + 1]
 
+    def couple(s, c):
+        for d in range(DEPTH):
+            z = layer_of(c, s, d)
+            squares = [jnp.square(field[s - 1, z * 10 + y + 1, 8:40, :]).astype(jnp.bfloat16) for y in range(COLS)]
+            sums[d] = jnp.dot(jnp.concatenate(squares, axis=0), pair_ref[...], preferred_element_type=jnp.float32)
+
     def step(s, c):
         def one(z, _):
             here = z * 10
             above = jnp.minimum(z + 1, LAYERS - 1) * 10
             below = jnp.maximum(z - 1, 0) * 10
-            squares = [jnp.square(field[s - 1, here + y + 1, 8:40, :]).astype(jnp.bfloat16) for y in range(COLS)]
-            twice = jnp.dot(jnp.concatenate(squares, axis=0), pair_ref[...], preferred_element_type=jnp.float32)
+            from_base = z - (c * DEPTH - s)
 
             def wide(n):
                 return jnp.concatenate([coef[n]] * 4, axis=0)
@@ -308,7 +315,7 @@
                 x_p, x_m = field[s - 1, here + y + 1, 9:41, :], field[s - 1, here + y + 1, 7:39, :]
                 y_p, y_m = field[s - 1, here + y + 2, 8:40, :], field[s - 1, here + y, 8:40, :]
                 z_p, z_m = field[s - 1, above + y + 1, 8:40, :], field[s - 1, below + y + 1, 8:40, :]
-                new = v * (a_0 - 0.1 * (v * v + twice[y * ROWS : (y + 1) * ROWS]))
+                new = v * (a_0 - 0.1 * (v * v + sums[from_base, y * ROWS : (y + 1) * ROWS, :]))
                 new = new + a_x * (x_p + x_m) + a_y * (y_p + y_m) + a_z * (z_p + z_m)
                 new = new + a_xy * (slopes[y + 2] - slopes[y])
                 at = z * COLS + y
@@ -331,6 +338,8 @@
             send_out[c, p : p + 4] = code.astype(jnp.int32).astype(jnp.int16)
 
     def first(c, _):
+        couple(1, c)
+
         @pl.when(c < CHUNKS)
         def _():
             take_rims(0, c)
@@ -340,12 +349,14 @@
         return 0
 
     def second(c, _):
+        couple(2, c)
         take_rims(1, c)
         step(2, c)
         send_rims(2, c)
         return 0
 
     def third(c, _):
+        couple(3, c)
         take_rims(2, c)
         step(3, c)
 
@@ -438,6 +449,7 @@
             pltpu.VMEM((PEERS * 32, 128), f32),
             pltpu.VMEM((4, LAYERS * 10, 48, 128), f32),
             pltpu.VMEM((3, LAYERS * COLS, ROWS, 128), f32),
+            pltpu.VMEM((DEPTH, COLS * ROWS, 128), f32),
             pltpu.VMEM((RIM_SLOTS, RIM_TOTAL, 128), bf16),
             pltpu.VMEM((RIM_SLOTS, RIM_TOTAL, 128), bf16),
             pltpu.VMEM((2, 8, 8, 128), f32),

time: 82.4 us -> 81.1 us (0.984)
  Pallas kernels: 78.8 us -> 77.5 us
    pallas_call x1, Pallas kernels: 78.8 us -> 77.5 us  [per_device(): pl.pallas_call(functools.partial(exchange_kernel, n_gx, n_gy), out_shape=...]
where the time goes in v3:
time: 81.1 us; the launch traced here: 81 us
  Pallas kernels  77.5 us (96%)
  other arithmetic  3.5 us (4%)
    pallas_call x1, Pallas kernels, per_device(): pl.pallas_call(functools.partial(exchange_kernel, n_gx, n_gy), out_shape=...  77.5 us
    select_n x1, other arithmetic, per_device(): return jnp.where(level < 0.0, -size, size)  3.5 us

profile of v3, /device:TPU:1, one launch (start us, length us, event | category | flops | bytes accessed | tf_op | source)
XLA Modules:
  0.0 81.0 jit_solution(7776972312924670243)
XLA Ops:
  0.0 77.5 %phase_steps.1 = s16[4,16,64,128]{3,2,1,0:T(8,128)(2,1)} custom-call(f32[4,16,64,128]{3,2,1,0:T(8,128)} %noise_hbm.1, s32[16,64,128]{2,1,0:T(8,128)} %labels_hbm.1, s32[128,128]{1,0:T(8,128)} %class_hbm.1, f32[4]{0:T(128)} %gain_hbm.1, f32[3,4]{1,0:T(4,128)} %stiff_hbm.1, f32[4]{0:T(128)} %cross_hbm.1, f32[3,16,64,128]{3,2,1,0:T(8,128)} %current_hbm.1), custom_call_target="tpu_custom_call" | custom-call | tf_op jit(solution)/shard_map/phase_steps/pallas_call | solution.py:431
  77.5 3.5 %negate_select_fusion = f32[4,16,64,128]{3,2,1,0:T(8,128)} fusion(s16[4,16,64,128]{3,2,1,0:T(8,128)(2,1)} %phase_steps.1), kind=kLoop, calls=%fused_computation | loop fusion | flops 4718592 | bytes 3145728 | tf_op jit(solution)/shard_map/jit(_where)/select_n | solution.py:477

commit v4 on v3

--- a/solution.py
+++ b/solution.py
@@ -22,6 +22,7 @@
 RIM_TOTAL = 384
 RIM_BASE = (0, 4, 9)
 RIM_SLOTS = 14
+HALF = 8
 
 
 def exchange_kernel(
@@ -163,7 +164,7 @@
         coef_first(k).start()
     pltpu.make_async_copy(coef_send.at[0], coef_recv.at[0, chip], coef_recv_sem.at[0]).start()
 
-    def swap(send, recv, send_sem, recv_sem, c):
+    def swap(send, recv, send_sem, recv_sem, c, low=1, high=PEERS):
         def one(k, _):
             to = (ga + k) % PEERS
             pltpu.make_async_remote_copy(
@@ -172,8 +173,9 @@
             ).start()
             return 0
 
-        lax.fori_loop(1, PEERS, one, 0)
-        pltpu.make_async_copy(send.at[c, ga], recv.at[c, ga], recv_sem.at[c]).start()
+        lax.fori_loop(low, high, one, 0)
+        if low == 1:
+            pltpu.make_async_copy(send.at[c, ga], recv.at[c, ga], recv_sem.at[c]).start()
 
     swap(send_in, recv_in, in_send_sem, in_recv_sem, 0)
     for c in range(1, CHUNKS):
@@ -390,8 +392,9 @@
     lax.fori_loop(3, CHUNKS + 1, first, 0)
     lax.fori_loop(2, 3, second, 0)
     lax.fori_loop(0, 2, third, 0)
+    swap(send_out, recv_out, out_send_sem, out_recv_sem, 0, 1, HALF)
     lax.fori_loop(3, CHUNKS + 1, second, 0)
-    swap(send_out, recv_out, out_send_sem, out_recv_sem, 0)
+    swap(send_out, recv_out, out_send_sem, out_recv_sem, 0, HALF, PEERS)
     lax.fori_loop(2, CHUNKS + 1, third, 0)
 
     def store(c):

time: 81.1 us -> 80.5 us (level)
  no operation moved by 1% of the time
where the time goes in v4:
time: 80.5 us; the launch traced here: 80.4 us
  Pallas kernels  76.9 us (96%)
  other arithmetic  3.5 us (4%)
    pallas_call x1, Pallas kernels, per_device(): pl.pallas_call(functools.partial(exchange_kernel, n_gx, n_gy), out_shape=...  76.9 us
    select_n x1, other arithmetic, per_device(): return jnp.where(level < 0.0, -size, size)  3.5 us

profile of v4, /device:TPU:1, one launch (start us, length us, event | category | flops | bytes accessed | tf_op | source)
XLA Modules:
  0.0 80.4 jit_solution(14118357945751334005)
XLA Ops:
  0.0 76.9 %phase_steps.1 = s16[4,16,64,128]{3,2,1,0:T(8,128)(2,1)} custom-call(f32[4,16,64,128]{3,2,1,0:T(8,128)} %noise_hbm.1, s32[16,64,128]{2,1,0:T(8,128)} %labels_hbm.1, s32[128,128]{1,0:T(8,128)} %class_hbm.1, f32[4]{0:T(128)} %gain_hbm.1, f32[3,4]{1,0:T(4,128)} %stiff_hbm.1, f32[4]{0:T(128)} %cross_hbm.1, f32[3,16,64,128]{3,2,1,0:T(8,128)} %current_hbm.1), custom_call_target="tpu_custom_call" | custom-call | tf_op jit(solution)/shard_map/phase_steps/pallas_call | solution.py:434
  76.9 3.5 %negate_select_fusion = f32[4,16,64,128]{3,2,1,0:T(8,128)} fusion(s16[4,16,64,128]{3,2,1,0:T(8,128)(2,1)} %phase_steps.1), kind=kLoop, calls=%fused_computation | loop fusion | flops 4718592 | bytes 3145728 | tf_op jit(solution)/shard_map/jit(_where)/select_n | solution.py:480
